TPU v7x, 256 devices: a whole 4x4x8 slice. The times are simulated.
256 devices in a mesh: wide: 32 (over z, x), narrow: 8 (over y, core).
Axes of the slice: x: 4, y: 4, z: 8, core: 2. Of those that a mesh axis runs over, the one named last changes fastest.
Arguments:
- cube: bfloat16 [256, 1536, 224], P('narrow', 'wide')
Outputs:
- restored: bfloat16 [256, 1536, 224], P('narrow', 'wide')
- projector: float32 [224, 224], replicated
All inputs are finite; a program needn't handle non-finite values.
Results may differ from a plain program's by a relative error of at most 0.0034.
Values may be sent and summed in bfloat16 or wider, within the bound.
A program may use at most 64 MiB of HBM per device.

v0:
```python
import jax
import jax.numpy as jnp
from jax import lax
from jax.sharding import PartitionSpec as P

TILE_ROWS = 32
TILE_COLS = 48
BANDS = 224
RANK = 16
POWER_ITERS = 4
TV_ITERS = 3
hi_prec = lax.Precision.HIGHEST


def with_halo(cells, sides, width):
    for axis, dim in sides:
        count = lax.axis_size(axis)
        ends = count - 1
        head = lax.slice_in_dim(cells, 0, width, axis=dim)
        tail = lax.slice_in_dim(cells, cells.shape[dim] - width, cells.shape[dim], axis=dim)
        cells = jnp.concatenate(
            [
                lax.ppermute(tail, axis, [(i, (i + 1) % count) for i in range(ends)]),
                cells,
                lax.ppermute(head, axis, [((i + 1) % count, i) for i in range(ends)]),
            ],
            axis=dim,
        )
    return cells


def smooth_step(field, fitted, grow, gcol, height, width):
    mask_x = ((grow >= 0) & (grow + 1 < height)).astype(jnp.float32)
    mask_y = ((gcol >= 0) & (gcol + 1 < width)).astype(jnp.float32)
    corner = field[:-1, :-1]
    grad_x = (field[1:, :-1] - corner) * mask_x[:-1, None, None]
    grad_y = (field[:-1, 1:] - corner) * mask_y[None, :-1, None]
    magnitude = jnp.sqrt(grad_x * grad_x + grad_y * grad_y + 0.25)
    flow_x = grad_x / magnitude
    flow_y = grad_y / magnitude
    diverg = flow_x[1:, 1:] - flow_x[:-1, 1:] + flow_y[1:, 1:] - flow_y[1:, :-1]
    centre = field[1:-1, 1:-1]
    return centre - 0.5 * (centre - fitted[1:-1, 1:-1] - 0.5 * diverg)


def subspace(gram):
    bands = lax.broadcasted_iota(jnp.float32, (BANDS, RANK), 0)
    cols = lax.broadcasted_iota(jnp.float32, (BANDS, RANK), 1)
    basis = jnp.cos(jnp.pi * (bands + 0.5) * cols / BANDS)
    for step in range(POWER_ITERS):
        grown = jnp.dot(gram, basis, precision=hi_prec)
        inner = jnp.dot(grown.T, grown, precision=hi_prec)
        lower = jnp.linalg.cholesky(inner)
        basis = jax.scipy.linalg.solve_triangular(lower, grown.T, lower=True).T
    return basis


def project_tile(block, basis, basis_low):
    loading = jnp.einsum("hwb,br->hwr", block, basis_low, preferred_element_type=jnp.float32)
    return jnp.einsum("hwr,br->hwb", loading, basis, precision=hi_prec)


def body(cube):
    n_rows = lax.axis_size("narrow")
    n_cols = lax.axis_size("wide")
    height = TILE_ROWS * n_rows
    width = TILE_COLS * n_cols
    row_base = lax.axis_index("narrow") * TILE_ROWS
    col_base = lax.axis_index("wide") * TILE_COLS
    flat = cube.reshape(TILE_ROWS * TILE_COLS, BANDS)
    local = lax.dot_general(
        flat, flat, (((0,), (0,)), ((), ())), preferred_element_type=jnp.float32
    )
    total = lax.psum(local, ("wide", "narrow"))
    gram = total / (height * width)
    basis = subspace(gram)
    projector = jnp.dot(basis, basis.T, precision=hi_prec)
    basis_low = basis.astype(jnp.bfloat16)
    fitted = project_tile(cube, basis, basis_low)
    fitted_pad = jnp.pad(fitted, ((1, 1), (1, 1), (0, 0)))
    rows = row_base - 1 + jnp.arange(TILE_ROWS + 2, dtype=jnp.int32)
    cols = col_base - 1 + jnp.arange(TILE_COLS + 2, dtype=jnp.int32)
    field = fitted
    for step in range(TV_ITERS):
        field_ext = with_halo(field, (("narrow", 0), ("wide", 1)), 1)
        field = smooth_step(field_ext, fitted_pad, rows, cols, height, width)
    return (field.astype(jnp.bfloat16), projector)


def solution(mesh):
    return jax.shard_map(
        body,
        mesh=mesh,
        in_specs=(P("narrow", "wide", None),),
        out_specs=(P("narrow", "wide", None), P()),
        check_vma=False,
    )
```

profile of v0, /device:TPU:111, one launch (start us, length us, event | category | flops | bytes accessed | tf_op | source)
XLA Modules:
  0.0 365.4 jit_solution(9770431130495249108)
XLA Ops:
  7.2 1.1 copy-done
  8.3 1.1 convolution_bitcast_fusion.1
  9.5 258.3 %all-reduce.2.cloned.1.call-done = f32[224,224]{1,0:T(8,128)} async-done(((f32[224,224]{1,0:T(8,128)}), f32[224,224]{1,0:T(8,128)}) %all-reduce.2.cloned.1.call-update) | async-done | bytes 200720 | tf_op jit(solution)/shard_map/psum | solution.py:74
  267.8 1.7 fusion.34
  269.5 0.1 fusion.84
  269.6 0.1 copy.3
  269.7 1.5 cholesky.74
  271.2 0.6 compare_reduce_fusion.3
  271.9 0.6 fusion.56
  272.5 1.2 custom-call.8
  273.7 0.2 fusion.54
  273.9 1.2 fusion.32
  275.1 0.2 fusion.85
  275.3 0.1 copy.4
  275.4 1.5 cholesky.85
  276.9 0.6 compare_reduce_fusion.2
  277.6 0.6 fusion.57
  278.2 1.2 custom-call.9
  279.4 0.2 fusion.52
  279.6 1.2 fusion.30
  280.9 0.2 fusion.86
  281.1 1.5 cholesky.96
  282.6 0.6 compare_reduce_fusion.1
  283.3 0.6 fusion.58
  283.9 1.2 custom-call.10
  285.2 0.2 fusion.50
  285.4 1.2 fusion.28
  286.6 0.2 fusion.87
  286.7 0.1 copy.6
  286.8 1.5 cholesky.107
  288.3 0.6 compare_reduce_fusion
  289.0 0.6 fusion.59
  289.6 1.2 custom-call.11
  290.9 0.2 fusion.48
  291.1 0.5 convolution_bitcast_fusion
  291.6 1.5 fusion.46
  293.1 1.9 collective-permute-start
  295.0 2.4 collective-permute-start.1
  297.4 3.0 collective-permute-done.1
  300.5 3.5 collective-permute-start.2
  304.0 1.9 collective-permute-start.3
  305.9 0.2 maximum_maximum_fusion
  306.1 5.9 %collective-permute-done.3 = f32[34,1,224]{2,1,0:T(1,128)S(1)} collective-permute-done((f32[34,1,224]{2,1,0:T(1,128)S(1)}, f32[34,1,224]{2,1,0:T(1,128)S(1)}, u32[]{:S(2)}, u32[]{:S(2)}) %collective-permute-start.3) | collective-permute-done | bytes 30496 | tf_op jit(solution)/shard_map/ppermute | solution.py:25
  312.0 1.4 fusion.14
  313.4 0.7 fusion.27
  314.1 3.5 collective-permute-start.4
  317.6 1.9 collective-permute-start.5
  319.5 3.5 collective-permute-done.5
  323.0 1.9 collective-permute-start.6
  325.0 3.4 collective-permute-start.7
  328.4 0.2 maximum_maximum_fusion.1
  328.6 4.4 %collective-permute-done.7 = f32[34,1,224]{2,1,0:T(1,128)S(1)} collective-permute-done((f32[34,1,224]{2,1,0:T(1,128)S(1)}, f32[34,1,224]{2,1,0:T(1,128)S(1)}, u32[]{:S(2)}, u32[]{:S(2)}) %collective-permute-start.7) | collective-permute-done | bytes 30496 | tf_op jit(solution)/shard_map/ppermute | solution.py:25
  333.0 1.4 fusion.12
  334.4 1.1 fusion.23
  335.5 3.1 collective-permute-start.8
  338.6 1.9 collective-permute-start.9
  340.5 3.5 collective-permute-done.9
  344.1 1.9 collective-permute-start.10
  346.0 1.1 fusion.88
  347.1 3.5 collective-permute-start.11
  350.6 0.2 maximum_maximum_fusion.2
  350.8 4.2 %collective-permute-done.11 = f32[34,1,224]{2,1,0:T(1,128)S(1)} collective-permute-done((f32[34,1,224]{2,1,0:T(1,128)S(1)}, f32[34,1,224]{2,1,0:T(1,128)S(1)}, u32[]{:S(2)}, u32[]{:S(2)}) %collective-permute-start.11) | collective-permute-done | bytes 30496 | tf_op jit(solution)/shard_map/ppermute | solution.py:25
  355.1 1.4 fusion.10
  356.5 2.0 fusion.19
  (29 shorter events, 0.5 us)
Async XLA Ops:
  7.2 1.1 copy-start
  7.2 260.6 %all-reduce.2.cloned.1.call-start = ((), (), s32[]{:S(2)}) async-start(), calls=%async_computation | async-start | bytes 458752 | tf_op jit(solution)/shard_map/psum | solution.py:74
  293.1 4.4 %collective-permute-start = (f32[1,48,224]{2,1,0:T(8,128)S(1)}, f32[1,48,224]{2,1,0:T(8,128)S(1)}, u32[]{:S(2)}, u32[]{:S(2)}) collective-permute-start(f32[1,48,224]{2,1,0:T(8,128)S(1)} %get-tuple-element.20), channel_id=1, source_target_pairs={{0,1},{1,2},{2,3},{3,4},{4,5},{5,6},{6,7},{8,9},{9,10},{10,11},{11... | collective-permute-start | bytes 129032 | tf_op jit(solution)/shard_map/ppermute | solution.py:23
  295.0 5.4 %collective-permute-start.1 = (f32[1,48,224]{2,1,0:T(8,128)S(1)}, f32[1,48,224]{2,1,0:T(8,128)S(1)}, u32[]{:S(2)}, u32[]{:S(2)}) collective-permute-start(f32[1,48,224]{2,1,0:T(8,128)S(1)} %get-tuple-element.21), channel_id=1, source_target_pairs={{1,0},{2,1},{3,2},{4,3},{5,4},{6,5},{7,6},{9,8},{10,9},{11,10},{12... | collective-permute-start | bytes 129032 | tf_op jit(solution)/shard_map/ppermute | solution.py:25
  300.5 5.5 %collective-permute-start.2 = (f32[34,1,224]{2,1,0:T(1,128)S(1)}, f32[34,1,224]{2,1,0:T(1,128)S(1)}, u32[]{:S(2)}, u32[]{:S(2)}) collective-permute-start(f32[34,1,224]{2,1,0:T(1,128)S(1)} %get-tuple-element.15), channel_id=1, source_target_pairs={{0,8},{8,16},{16,24},{24,32},{32,40},{40,48},{48,56},{56,64},{64,7... | collective-permute-start | bytes 91400 | tf_op jit(solution)/shard_map/ppermute | solution.py:23
  304.0 8.0 %collective-permute-start.3 = (f32[34,1,224]{2,1,0:T(1,128)S(1)}, f32[34,1,224]{2,1,0:T(1,128)S(1)}, u32[]{:S(2)}, u32[]{:S(2)}) collective-permute-start(f32[34,1,224]{2,1,0:T(1,128)S(1)} %get-tuple-element.14), channel_id=1, source_target_pairs={{8,0},{16,8},{24,16},{32,24},{40,32},{48,40},{56,48},{64,56},{72,6... | collective-permute-start | bytes 91400 | tf_op jit(solution)/shard_map/ppermute | solution.py:25
  314.1 5.4 %collective-permute-start.4 = (f32[1,48,224]{2,1,0:T(8,128)S(1)}, f32[1,48,224]{2,1,0:T(8,128)S(1)}, u32[]{:S(2)}, u32[]{:S(2)}) collective-permute-start(f32[1,48,224]{2,1,0:T(8,128)S(1)} %get-tuple-element.18), channel_id=1, source_target_pairs={{0,1},{1,2},{2,3},{3,4},{4,5},{5,6},{6,7},{8,9},{9,10},{10,11},{11... | collective-permute-start | bytes 129032 | tf_op jit(solution)/shard_map/ppermute | solution.py:23
  317.6 5.4 %collective-permute-start.5 = (f32[1,48,224]{2,1,0:T(8,128)S(1)}, f32[1,48,224]{2,1,0:T(8,128)S(1)}, u32[]{:S(2)}, u32[]{:S(2)}) collective-permute-start(f32[1,48,224]{2,1,0:T(8,128)S(1)} %get-tuple-element.19), channel_id=1, source_target_pairs={{1,0},{2,1},{3,2},{4,3},{5,4},{6,5},{7,6},{9,8},{10,9},{11,10},{12... | collective-permute-start | bytes 129032 | tf_op jit(solution)/shard_map/ppermute | solution.py:25
  323.0 5.3 %collective-permute-start.6 = (f32[34,1,224]{2,1,0:T(1,128)S(1)}, f32[34,1,224]{2,1,0:T(1,128)S(1)}, u32[]{:S(2)}, u32[]{:S(2)}) collective-permute-start(f32[34,1,224]{2,1,0:T(1,128)S(1)} %get-tuple-element.13), channel_id=1, source_target_pairs={{0,8},{8,16},{16,24},{24,32},{32,40},{40,48},{48,56},{56,64},{64,7... | collective-permute-start | bytes 91400 | tf_op jit(solution)/shard_map/ppermute | solution.py:23
  325.0 8.0 %collective-permute-start.7 = (f32[34,1,224]{2,1,0:T(1,128)S(1)}, f32[34,1,224]{2,1,0:T(1,128)S(1)}, u32[]{:S(2)}, u32[]{:S(2)}) collective-permute-start(f32[34,1,224]{2,1,0:T(1,128)S(1)} %get-tuple-element.12), channel_id=1, source_target_pairs={{8,0},{16,8},{24,16},{32,24},{40,32},{48,40},{56,48},{64,56},{72,6... | collective-permute-start | bytes 91400 | tf_op jit(solution)/shard_map/ppermute | solution.py:25
  335.5 5.1 %collective-permute-start.8 = (f32[1,48,224]{2,1,0:T(8,128)S(1)}, f32[1,48,224]{2,1,0:T(8,128)S(1)}, u32[]{:S(2)}, u32[]{:S(2)}) collective-permute-start(f32[1,48,224]{2,1,0:T(8,128)S(1)} %get-tuple-element.16), channel_id=1, source_target_pairs={{0,1},{1,2},{2,3},{3,4},{4,5},{5,6},{6,7},{8,9},{9,10},{10,11},{11... | collective-permute-start | bytes 129032 | tf_op jit(solution)/shard_map/ppermute | solution.py:23
  338.6 5.4 %collective-permute-start.9 = (f32[1,48,224]{2,1,0:T(8,128)S(1)}, f32[1,48,224]{2,1,0:T(8,128)S(1)}, u32[]{:S(2)}, u32[]{:S(2)}) collective-permute-start(f32[1,48,224]{2,1,0:T(8,128)S(1)} %get-tuple-element.17), channel_id=1, source_target_pairs={{1,0},{2,1},{3,2},{4,3},{5,4},{6,5},{7,6},{9,8},{10,9},{11,10},{12... | collective-permute-start | bytes 129032 | tf_op jit(solution)/shard_map/ppermute | solution.py:25
  344.1 6.5 %collective-permute-start.10 = (f32[34,1,224]{2,1,0:T(1,128)S(1)}, f32[34,1,224]{2,1,0:T(1,128)S(1)}, u32[]{:S(2)}, u32[]{:S(2)}) collective-permute-start(f32[34,1,224]{2,1,0:T(1,128)S(1)} %get-tuple-element.11), channel_id=1, source_target_pairs={{0,8},{8,16},{16,24},{24,32},{32,40},{40,48},{48,56},{56,64},{64,7... | collective-permute-start | bytes 91400 | tf_op jit(solution)/shard_map/ppermute | solution.py:23
  347.1 8.0 %collective-permute-start.11 = (f32[34,1,224]{2,1,0:T(1,128)S(1)}, f32[34,1,224]{2,1,0:T(1,128)S(1)}, u32[]{:S(2)}, u32[]{:S(2)}) collective-permute-start(f32[34,1,224]{2,1,0:T(1,128)S(1)} %get-tuple-element.10), channel_id=1, source_target_pairs={{8,0},{16,8},{24,16},{32,24},{40,32},{48,40},{56,48},{64,56},{72,6... | collective-permute-start | bytes 91400 | tf_op jit(solution)/shard_map/ppermute | solution.py:25
Sparse Core Ops, SparseCore 0:
  14.1 253.6 all-reduce.1
where the time goes:
time: 366 us; the launch traced here: 365 us
  waiting for transfers between devices  283 us (77%)
  starting transfers between devices  31 us (8%)
  other arithmetic  24.9 us (7%)
  between operations  14.4 us (4%)
  matrix products  10.9 us (3%)
    psum x1, waiting for transfers between devices, body(): total = lax.psum(local, ('wide', 'narrow'))  258 us
    ppermute x6, waiting for transfers between devices, with_halo(): lax.ppermute(head, axis, [((i + 1) % count, i) for i in range(ends)])  24.4 us
    ppermute x6, starting transfers between devices, with_halo(): lax.ppermute(tail, axis, [(i, (i + 1) % count) for i in range(ends)])  15.9 us
    ppermute x6, starting transfers between devices, with_halo(): lax.ppermute(head, axis, [((i + 1) % count, i) for i in range(ends)])  15.1 us
    another operation x12, other arithmetic, subspace(): lower = jnp.linalg.cholesky(inner)  8.57 us
    another operation x8, other arithmetic, subspace(): basis = jax.scipy.linalg.solve_triangular(lower, grown.T, lower=True).T  7.51 us
  transfers between devices with their start and end apart: 13, of which 7 were waited for; matrix products, arithmetic and copies ran while one was open for 0% of the time, Pallas kernels for 0%

commit v1 on v0

--- a/solution.py
+++ b/solution.py
@@ -71,7 +71,7 @@
     local = lax.dot_general(
         flat, flat, (((0,), (0,)), ((), ())), preferred_element_type=jnp.float32
     )
-    total = lax.psum(local, ("wide", "narrow"))
+    total = jnp.sum(lax.all_gather(local, ("wide", "narrow")), axis=0)
     gram = total / (height * width)
     basis = subspace(gram)
     projector = jnp.dot(basis, basis.T, precision=hi_prec)

time: 366 us -> 324 us (0.89)
  waiting for transfers between devices: 283 us -> 224 us
  other arithmetic: 24.9 us -> 43.8 us
  matrix products: 10.9 us -> 7.14 us
    psum x1 -> x0, waiting for transfers between devices: 258 us -> none  [body(): total = lax.psum(local, ('wide', 'narrow'))]
    all_gather x0 -> x1, waiting for transfers between devices: none -> 199 us  [body(): total = jnp.sum(lax.all_gather(local, ('wide', 'narrow')), axis=0)]
    reduce_sum x0 -> x1, other arithmetic: none -> 18.6 us  [body(): total = jnp.sum(lax.all_gather(local, ('wide', 'narrow')), axis=0)]
    dot_general x4, matrix products: 5.3 us -> 1.54 us  [subspace(): grown = jnp.dot(gram, basis, precision=hi_prec)]
  transfers between devices with their start and end apart: 13 -> 13, of which waited for: 7 -> 7; matrix products, arithmetic and copies ran while one was open for 0% -> 1% of each run, Pallas kernels for 0% -> 0%
where the time goes in v1:
time: 324 us; the launch traced here: 323 us
  waiting for transfers between devices  224 us (69%)
  other arithmetic  43.8 us (14%)
  starting transfers between devices  32.6 us (10%)
  between operations  14.4 us (4%)
  matrix products  7.14 us (2%)
    all_gather x1, waiting for transfers between devices, body(): total = jnp.sum(lax.all_gather(local, ('wide', 'narrow')), axis=0)  199 us
    ppermute x6, waiting for transfers between devices, with_halo(): lax.ppermute(head, axis, [((i + 1) % count, i) for i in range(ends)])  24.9 us
    reduce_sum x1, other arithmetic, body(): total = jnp.sum(lax.all_gather(local, ('wide', 'narrow')), axis=0)  18.6 us
    ppermute x6, starting transfers between devices, with_halo(): lax.ppermute(tail, axis, [(i, (i + 1) % count) for i in range(ends)])  18 us
    ppermute x6, starting transfers between devices, with_halo(): lax.ppermute(head, axis, [((i + 1) % count, i) for i in range(ends)])  14.6 us
    another operation x12, other arithmetic, subspace(): lower = jnp.linalg.cholesky(inner)  8.57 us
    another operation x8, other arithmetic, subspace(): basis = jax.scipy.linalg.solve_triangular(lower, grown.T, lower=True).T  7.51 us
  transfers between devices with their start and end apart: 13, of which 7 were waited for; matrix products, arithmetic and copies ran while one was open for 1% of the time, Pallas kernels for 0%

profile of v1, /device:TPU:111, one launch (start us, length us, event | category | flops | bytes accessed | tf_op | source)
XLA Modules:
  0.0 323.1 jit_solution(309271315938001995)
XLA Ops:
  7.2 1.1 copy-done
  8.3 1.1 convolution_bitcast_fusion.1
  9.5 198.8 %all-gather.3.cloned.1.call-done = f32[57344,224]{1,0:T(8,128)} async-done(((f32[224,224]{1,0:T(8,128)}), f32[57344,224]{1,0:T(8,128)}) %all-gather.3.cloned.1.call-update) | async-done | bytes 51380240 | tf_op jit(solution)/shard_map/all_gather | solution.py:74
  208.3 18.6 %reduce_sum.9 = f32[224,224]{1,0:T(8,128)S(1)} reduce(f32[256,224,224]{2,1,0:T(8,128)} %bitcast.76, f32[]{:T(128)} %constant.58.clone.1), dimensions={0}, to_apply=%region_0.0 | reduce | flops 12794880 | bytes 51580932 | tf_op jit(solution)/shard_map/reduce_sum | solution.py:74
  226.9 0.7 fusion.34
  227.7 0.1 fusion.84
  227.9 1.5 cholesky.74
  229.4 0.6 compare_reduce_fusion.3
  230.0 0.6 fusion.56
  230.7 1.2 custom-call.8
  231.9 0.2 fusion.54
  232.1 0.3 fusion.32
  232.4 0.2 fusion.85
  232.7 1.5 cholesky.85
  234.2 0.6 compare_reduce_fusion.2
  234.8 0.6 fusion.57
  235.5 1.2 custom-call.9
  236.7 0.2 fusion.52
  236.9 0.3 fusion.30
  237.2 0.2 fusion.86
  237.4 0.1 copy.5
  237.5 1.5 cholesky.96
  238.9 0.6 compare_reduce_fusion.1
  239.6 0.6 fusion.58
  240.3 1.2 custom-call.10
  241.5 0.2 fusion.50
  241.7 0.3 fusion.28
  242.0 0.2 fusion.87
  242.1 0.1 copy.6
  242.2 1.5 cholesky.107
  243.7 0.6 compare_reduce_fusion
  244.4 0.6 fusion.59
  245.0 1.2 custom-call.11
  246.3 0.2 fusion.48
  246.5 0.5 convolution_bitcast_fusion
  246.9 1.5 fusion.46
  248.4 3.0 collective-permute-start
  251.5 1.9 collective-permute-start.1
  253.4 3.5 %collective-permute-done.1 = f32[1,48,224]{2,1,0:T(8,128)S(1)} collective-permute-done((f32[1,48,224]{2,1,0:T(8,128)S(1)}, f32[1,48,224]{2,1,0:T(8,128)S(1)}, u32[]{:S(2)}, u32[]{:S(2)}) %collective-permute-start.1) | collective-permute-done | bytes 43040 | tf_op jit(solution)/shard_map/ppermute | solution.py:25
  257.0 4.1 %collective-permute-start.2 = (f32[34,1,224]{2,1,0:T(1,128)S(1)}, f32[34,1,224]{2,1,0:T(1,128)S(1)}, u32[]{:S(2)}, u32[]{:S(2)}) collective-permute-start(f32[34,1,224]{2,1,0:T(1,128)S(1)} %get-tuple-element.15), channel_id=1, source_target_pairs={{0,8},{8,16},{16,24},{24,32},{32,40},{40,48},{48,56},{56,64},{64,7... | collective-permute-start | bytes 91400 | tf_op jit(solution)/shard_map/ppermute | solution.py:23
  261.1 1.9 collective-permute-start.3
  263.0 0.2 maximum_maximum_fusion
  263.2 5.9 %collective-permute-done.3 = f32[34,1,224]{2,1,0:T(1,128)S(1)} collective-permute-done((f32[34,1,224]{2,1,0:T(1,128)S(1)}, f32[34,1,224]{2,1,0:T(1,128)S(1)}, u32[]{:S(2)}, u32[]{:S(2)}) %collective-permute-start.3) | collective-permute-done | bytes 30496 | tf_op jit(solution)/shard_map/ppermute | solution.py:25
  269.1 1.4 fusion.14
  270.5 0.9 fusion.27
  271.4 3.6 %collective-permute-start.4 = (f32[1,48,224]{2,1,0:T(8,128)S(1)}, f32[1,48,224]{2,1,0:T(8,128)S(1)}, u32[]{:S(2)}, u32[]{:S(2)}) collective-permute-start(f32[1,48,224]{2,1,0:T(8,128)S(1)} %get-tuple-element.18), channel_id=1, source_target_pairs={{0,1},{1,2},{2,3},{3,4},{4,5},{5,6},{6,7},{8,9},{9,10},{10,11},{11... | collective-permute-start | bytes 129032 | tf_op jit(solution)/shard_map/ppermute | solution.py:23
  275.1 1.9 collective-permute-start.5
  277.0 3.5 %collective-permute-done.5 = f32[1,48,224]{2,1,0:T(8,128)S(1)} collective-permute-done((f32[1,48,224]{2,1,0:T(8,128)S(1)}, f32[1,48,224]{2,1,0:T(8,128)S(1)}, u32[]{:S(2)}, u32[]{:S(2)}) %collective-permute-start.5) | collective-permute-done | bytes 43040 | tf_op jit(solution)/shard_map/ppermute | solution.py:25
  280.5 1.9 collective-permute-start.6
  282.5 3.4 %collective-permute-start.7 = (f32[34,1,224]{2,1,0:T(1,128)S(1)}, f32[34,1,224]{2,1,0:T(1,128)S(1)}, u32[]{:S(2)}, u32[]{:S(2)}) collective-permute-start(f32[34,1,224]{2,1,0:T(1,128)S(1)} %get-tuple-element.12), channel_id=1, source_target_pairs={{8,0},{16,8},{24,16},{32,24},{40,32},{48,40},{56,48},{64,56},{72,6... | collective-permute-start | bytes 91400 | tf_op jit(solution)/shard_map/ppermute | solution.py:25
  285.8 0.2 maximum_maximum_fusion.1
  286.1 4.4 %collective-permute-done.7 = f32[34,1,224]{2,1,0:T(1,128)S(1)} collective-permute-done((f32[34,1,224]{2,1,0:T(1,128)S(1)}, f32[34,1,224]{2,1,0:T(1,128)S(1)}, u32[]{:S(2)}, u32[]{:S(2)}) %collective-permute-start.7) | collective-permute-done | bytes 30496 | tf_op jit(solution)/shard_map/ppermute | solution.py:25
  290.5 1.4 fusion.12
  291.9 1.1 fusion.23
  293.0 3.4 %collective-permute-start.8 = (f32[1,48,224]{2,1,0:T(8,128)S(1)}, f32[1,48,224]{2,1,0:T(8,128)S(1)}, u32[]{:S(2)}, u32[]{:S(2)}) collective-permute-start(f32[1,48,224]{2,1,0:T(8,128)S(1)} %get-tuple-element.16), channel_id=1, source_target_pairs={{0,1},{1,2},{2,3},{3,4},{4,5},{5,6},{6,7},{8,9},{9,10},{10,11},{11... | collective-permute-start | bytes 129032 | tf_op jit(solution)/shard_map/ppermute | solution.py:23
  296.3 1.9 collective-permute-start.9
  298.3 3.5 %collective-permute-done.9 = f32[1,48,224]{2,1,0:T(8,128)S(1)} collective-permute-done((f32[1,48,224]{2,1,0:T(8,128)S(1)}, f32[1,48,224]{2,1,0:T(8,128)S(1)}, u32[]{:S(2)}, u32[]{:S(2)}) %collective-permute-start.9) | collective-permute-done | bytes 43040 | tf_op jit(solution)/shard_map/ppermute | solution.py:25
  301.8 1.9 collective-permute-start.10
  303.7 1.1 fusion.88
  304.8 3.5 %collective-permute-start.11 = (f32[34,1,224]{2,1,0:T(1,128)S(1)}, f32[34,1,224]{2,1,0:T(1,128)S(1)}, u32[]{:S(2)}, u32[]{:S(2)}) collective-permute-start(f32[34,1,224]{2,1,0:T(1,128)S(1)} %get-tuple-element.10), channel_id=1, source_target_pairs={{8,0},{16,8},{24,16},{32,24},{40,32},{48,40},{56,48},{64,56},{72,6... | collective-permute-start | bytes 91400 | tf_op jit(solution)/shard_map/ppermute | solution.py:25
  308.3 0.2 maximum_maximum_fusion.2
  308.5 4.2 %collective-permute-done.11 = f32[34,1,224]{2,1,0:T(1,128)S(1)} collective-permute-done((f32[34,1,224]{2,1,0:T(1,128)S(1)}, f32[34,1,224]{2,1,0:T(1,128)S(1)}, u32[]{:S(2)}, u32[]{:S(2)}) %collective-permute-start.11) | collective-permute-done | bytes 30496 | tf_op jit(solution)/shard_map/ppermute | solution.py:25
  312.8 1.4 fusion.10
  314.2 2.0 fusion.19
  (32 shorter events, 0.6 us)
Async XLA Ops:
  7.2 1.1 copy-start
  7.2 201.1 %all-gather.3.cloned.1.call-start = ((), (), s32[]{:S(2)}) async-start(), calls=%async_computation | async-start | bytes 58949632 | tf_op jit(solution)/shard_map/all_gather | solution.py:74
  248.4 5.0 %collective-permute-start = (f32[1,48,224]{2,1,0:T(8,128)S(1)}, f32[1,48,224]{2,1,0:T(8,128)S(1)}, u32[]{:S(2)}, u32[]{:S(2)}) collective-permute-start(f32[1,48,224]{2,1,0:T(8,128)S(1)} %get-tuple-element.20), channel_id=1, source_target_pairs={{0,1},{1,2},{2,3},{3,4},{4,5},{5,6},{6,7},{8,9},{9,10},{10,11},{11... | collective-permute-start | bytes 129032 | tf_op jit(solution)/shard_map/ppermute | solution.py:23
  251.5 5.4 %collective-permute-start.1 = (f32[1,48,224]{2,1,0:T(8,128)S(1)}, f32[1,48,224]{2,1,0:T(8,128)S(1)}, u32[]{:S(2)}, u32[]{:S(2)}) collective-permute-start(f32[1,48,224]{2,1,0:T(8,128)S(1)} %get-tuple-element.21), channel_id=1, source_target_pairs={{1,0},{2,1},{3,2},{4,3},{5,4},{6,5},{7,6},{9,8},{10,9},{11,10},{12... | collective-permute-start | bytes 129032 | tf_op jit(solution)/shard_map/ppermute | solution.py:25
  257.0 6.1 %collective-permute-start.2 = (f32[34,1,224]{2,1,0:T(1,128)S(1)}, f32[34,1,224]{2,1,0:T(1,128)S(1)}, u32[]{:S(2)}, u32[]{:S(2)}) collective-permute-start(f32[34,1,224]{2,1,0:T(1,128)S(1)} %get-tuple-element.15), channel_id=1, source_target_pairs={{0,8},{8,16},{16,24},{24,32},{32,40},{40,48},{48,56},{56,64},{64,7... | collective-permute-start | bytes 91400 | tf_op jit(solution)/shard_map/ppermute | solution.py:23
  261.1 8.0 %collective-permute-start.3 = (f32[34,1,224]{2,1,0:T(1,128)S(1)}, f32[34,1,224]{2,1,0:T(1,128)S(1)}, u32[]{:S(2)}, u32[]{:S(2)}) collective-permute-start(f32[34,1,224]{2,1,0:T(1,128)S(1)} %get-tuple-element.14), channel_id=1, source_target_pairs={{8,0},{16,8},{24,16},{32,24},{40,32},{48,40},{56,48},{64,56},{72,6... | collective-permute-start | bytes 91400 | tf_op jit(solution)/shard_map/ppermute | solution.py:25
  271.4 5.6 %collective-permute-start.4 = (f32[1,48,224]{2,1,0:T(8,128)S(1)}, f32[1,48,224]{2,1,0:T(8,128)S(1)}, u32[]{:S(2)}, u32[]{:S(2)}) collective-permute-start(f32[1,48,224]{2,1,0:T(8,128)S(1)} %get-tuple-element.18), channel_id=1, source_target_pairs={{0,1},{1,2},{2,3},{3,4},{4,5},{5,6},{6,7},{8,9},{9,10},{10,11},{11... | collective-permute-start | bytes 129032 | tf_op jit(solution)/shard_map/ppermute | solution.py:23
  275.1 5.4 %collective-permute-start.5 = (f32[1,48,224]{2,1,0:T(8,128)S(1)}, f32[1,48,224]{2,1,0:T(8,128)S(1)}, u32[]{:S(2)}, u32[]{:S(2)}) collective-permute-start(f32[1,48,224]{2,1,0:T(8,128)S(1)} %get-tuple-element.19), channel_id=1, source_target_pairs={{1,0},{2,1},{3,2},{4,3},{5,4},{6,5},{7,6},{9,8},{10,9},{11,10},{12... | collective-permute-start | bytes 129032 | tf_op jit(solution)/shard_map/ppermute | solution.py:25
  280.5 5.3 %collective-permute-start.6 = (f32[34,1,224]{2,1,0:T(1,128)S(1)}, f32[34,1,224]{2,1,0:T(1,128)S(1)}, u32[]{:S(2)}, u32[]{:S(2)}) collective-permute-start(f32[34,1,224]{2,1,0:T(1,128)S(1)} %get-tuple-element.13), channel_id=1, source_target_pairs={{0,8},{8,16},{16,24},{24,32},{32,40},{40,48},{48,56},{56,64},{64,7... | collective-permute-start | bytes 91400 | tf_op jit(solution)/shard_map/ppermute | solution.py:23
  282.5 8.0 %collective-permute-start.7 = (f32[34,1,224]{2,1,0:T(1,128)S(1)}, f32[34,1,224]{2,1,0:T(1,128)S(1)}, u32[]{:S(2)}, u32[]{:S(2)}) collective-permute-start(f32[34,1,224]{2,1,0:T(1,128)S(1)} %get-tuple-element.12), channel_id=1, source_target_pairs={{8,0},{16,8},{24,16},{32,24},{40,32},{48,40},{56,48},{64,56},{72,6... | collective-permute-start | bytes 91400 | tf_op jit(solution)/shard_map/ppermute | solution.py:25
  293.0 5.3 %collective-permute-start.8 = (f32[1,48,224]{2,1,0:T(8,128)S(1)}, f32[1,48,224]{2,1,0:T(8,128)S(1)}, u32[]{:S(2)}, u32[]{:S(2)}) collective-permute-start(f32[1,48,224]{2,1,0:T(8,128)S(1)} %get-tuple-element.16), channel_id=1, source_target_pairs={{0,1},{1,2},{2,3},{3,4},{4,5},{5,6},{6,7},{8,9},{9,10},{10,11},{11... | collective-permute-start | bytes 129032 | tf_op jit(solution)/shard_map/ppermute | solution.py:23
  296.3 5.4 %collective-permute-start.9 = (f32[1,48,224]{2,1,0:T(8,128)S(1)}, f32[1,48,224]{2,1,0:T(8,128)S(1)}, u32[]{:S(2)}, u32[]{:S(2)}) collective-permute-start(f32[1,48,224]{2,1,0:T(8,128)S(1)} %get-tuple-element.17), channel_id=1, source_target_pairs={{1,0},{2,1},{3,2},{4,3},{5,4},{6,5},{7,6},{9,8},{10,9},{11,10},{12... | collective-permute-start | bytes 129032 | tf_op jit(solution)/shard_map/ppermute | solution.py:25
  301.8 6.5 %collective-permute-start.10 = (f32[34,1,224]{2,1,0:T(1,128)S(1)}, f32[34,1,224]{2,1,0:T(1,128)S(1)}, u32[]{:S(2)}, u32[]{:S(2)}) collective-permute-start(f32[34,1,224]{2,1,0:T(1,128)S(1)} %get-tuple-element.11), channel_id=1, source_target_pairs={{0,8},{8,16},{16,24},{24,32},{32,40},{40,48},{48,56},{56,64},{64,7... | collective-permute-start | bytes 91400 | tf_op jit(solution)/shard_map/ppermute | solution.py:23
  304.8 8.0 %collective-permute-start.11 = (f32[34,1,224]{2,1,0:T(1,128)S(1)}, f32[34,1,224]{2,1,0:T(1,128)S(1)}, u32[]{:S(2)}, u32[]{:S(2)}) collective-permute-start(f32[34,1,224]{2,1,0:T(1,128)S(1)} %get-tuple-element.10), channel_id=1, source_target_pairs={{8,0},{16,8},{24,16},{32,24},{40,32},{48,40},{56,48},{64,56},{72,6... | collective-permute-start | bytes 91400 | tf_op jit(solution)/shard_map/ppermute | solution.py:25
  314.2 2.0 copy-start.1
Sparse Core Ops, SparseCore 0:
  12.1 196.1 all-gather.2
